TPU v7x, 32 devices: a whole 2x2x4 slice. The times are simulated.
32 devices in a mesh: groups: 2 (over y), ctx: 4 (over z), chan: 4 (over x, core).
Axes of the slice: x: 2, y: 2, z: 4, core: 2. Of those that a mesh axis runs over, the one named last changes fastest.
Arguments:
- query_gate: float32 [4096, 1024], P(('groups', 'ctx'), 'chan'), parts along dimension 0, may hold values from -6 to 6
- key_gate: float32 [4096, 1024], P(('groups', 'ctx'), 'chan'), parts along dimension 0, may hold values from -6 to 6
- values: float32 [4096, 1024], P(('groups', 'ctx'), 'chan'), parts along dimension 0, may hold values from -6 to 6
- filter_taps: float32 [4096, 1024], P(None, 'chan'), may hold values from -0.125 to 0.125
- skip_gain: float32 [1024], P('chan'), may hold values from -1 to 1
- upstream: float32 [4096, 1024], P(('groups', 'ctx'), 'chan'), parts along dimension 0, may hold values from -6 to 6
Outputs:
- query_grad: float32 [4096, 1024], P(('groups', 'ctx'), 'chan'), parts along dimension 0
- key_grad: float32 [4096, 1024], P(('groups', 'ctx'), 'chan'), parts along dimension 0
- value_grad: float32 [4096, 1024], P(('groups', 'ctx'), 'chan'), parts along dimension 0
- filter_grad: float32 [8192, 1024], P(('groups', 'ctx'), 'chan'), parts along dimension 0
- skip_grad: float32 [2048], P(('groups', 'chan')), parts along dimension 0
There are 2 independent parts, one for each index of `groups`. A program takes and returns all parts, laid end to end along the dimension named above; an argument that names none is the same for every part. Nothing has to cross between parts.
All inputs are finite; a program needn't handle non-finite values.
Results may differ from a plain program's by a relative error of at most 0.0001.
Values sent between devices are 32-bit elements; how exact they have to be, the bound alone decides.
No kernel may reach another device: no remote copies, remote signals or barrier semaphores. Data moves between devices by JAX's collectives and lax.ppermute only.
A program may use at most 128 MiB of HBM per device.

v0:
```python
import math
import jax
import jax.numpy as jnp
from jax import lax
from jax.sharding import PartitionSpec as P


def matmul(left, right):
    return jnp.dot(left, right, preferred_element_type=jnp.float32, precision=lax.Precision.HIGHEST)


def forward_table(seg_len, count, offset):
    num_bins = seg_len + 1
    period = 2 * seg_len
    bin_index = lax.broadcasted_iota(jnp.int32, (num_bins, count), 0)
    pos_index = lax.broadcasted_iota(jnp.int32, (num_bins, count), 1) + offset
    angles = (bin_index * pos_index % period).astype(jnp.float32) * (2.0 * math.pi / period)
    return jnp.concatenate([jnp.cos(angles), -jnp.sin(angles)], axis=0)


def inverse_table(seg_len, count, offset):
    num_bins = seg_len + 1
    period = 2 * seg_len
    pos_index = lax.broadcasted_iota(jnp.int32, (count, num_bins), 0) + offset
    bin_index = lax.broadcasted_iota(jnp.int32, (count, num_bins), 1)
    angles = (bin_index * pos_index % period).astype(jnp.float32) * (2.0 * math.pi / period)
    weights = jnp.where((bin_index == 0) | (bin_index == seg_len), 1.0, 2.0) / period
    return jnp.concatenate([weights * jnp.cos(angles), -weights * jnp.sin(angles)], axis=1)


def times_spec(first, second):
    num_bins = first.shape[0] // 2
    real_a, imag_a = (first[:num_bins], first[num_bins:])
    real_b, imag_b = (second[:num_bins], second[num_bins:])
    return jnp.concatenate(
        [real_a * real_b - imag_a * imag_b, real_a * imag_b + imag_a * real_b], axis=0
    )


def conj_times(first, second):
    num_bins = first.shape[0] // 2
    real_a, imag_a = (first[:num_bins], first[num_bins:])
    real_b, imag_b = (second[:num_bins], second[num_bins:])
    return jnp.concatenate(
        [real_a * real_b + imag_a * imag_b, real_a * imag_b - imag_a * real_b], axis=0
    )


def pick(stack, index):
    return lax.dynamic_index_in_dim(stack, index, 0, keepdims=False)


def local(query_gate, key_gate, values, filter_taps, skip_gain, upstream):
    seg_len, width_dev = values.shape
    cycle_size = lax.axis_size("ctx")
    position = lax.axis_index("ctx")
    history = seg_len * cycle_size
    gated = key_gate * values
    mixed_grad = upstream * query_gate
    table_low = forward_table(seg_len, seg_len, 0)
    table_high = forward_table(seg_len, seg_len, seg_len)
    table_taps = forward_table(seg_len, 2 * seg_len, 0)
    back_low = inverse_table(seg_len, seg_len, 0)
    back_high = inverse_table(seg_len, seg_len, seg_len)
    back_full = inverse_table(seg_len, 2 * seg_len, 0)
    own_grad_spec = matmul(table_high, mixed_grad)
    spec_rows = 2 * (seg_len + 1)

    def taps_spec(lag_block):
        start_row = (lag_block - 1) * seg_len + history
        window = lax.dynamic_slice_in_dim(filter_taps, start_row, 2 * seg_len, 0)
        return matmul(table_taps, window)

    def visit(carry, gated_spec, grad_spec, source):
        acc_conv, acc_back, partial_value = carry
        lag_block = position - source
        acc_conv = acc_conv + times_spec(taps_spec(lag_block), gated_spec)
        acc_back = acc_back + conj_times(taps_spec(-lag_block), grad_spec)
        segment = matmul(back_full, conj_times(gated_spec, own_grad_spec))
        start_row = (lag_block - 1) * seg_len + history
        current = lax.dynamic_slice_in_dim(partial_value, start_row, 2 * seg_len, 0)
        partial_value = lax.dynamic_update_slice_in_dim(
            partial_value, current + segment, start_row, 0
        )
        return (acc_conv, acc_back, partial_value)

    initial = (
        jnp.zeros((spec_rows, width_dev), jnp.float32),
        jnp.zeros((spec_rows, width_dev), jnp.float32),
        jnp.zeros((2 * history, width_dev), jnp.float32),
    )
    own_gated_spec = matmul(table_low, gated)
    pieces = (
        lax.all_gather(own_gated_spec[None], "ctx", axis=0, tiled=True),
        lax.all_gather(own_grad_spec[None], "ctx", axis=0, tiled=True),
    )

    def advance(member, state):
        return visit(state, pick(pieces[0], member), pick(pieces[1], member), member)

    folded = lax.fori_loop(0, pieces[0].shape[0], advance, initial)
    acc_conv, acc_back, partial_value = folded
    filter_grad = lax.psum_scatter(partial_value, "ctx", scatter_dimension=0, tiled=True)
    conv = matmul(back_high, acc_conv)
    back = matmul(back_low, acc_back) + skip_gain[None, :] * mixed_grad
    query_grad = upstream * (conv + skip_gain[None, :] * gated)
    key_grad = back * values
    value_grad = back * key_gate
    skip_grad = lax.psum(jnp.sum(mixed_grad * gated, axis=0), "ctx")
    return (query_grad, key_grad, value_grad, filter_grad, skip_grad)


def solution(mesh):
    in_specs = (
        P(("groups", "ctx"), "chan"),
        P(("groups", "ctx"), "chan"),
        P(("groups", "ctx"), "chan"),
        P(None, "chan"),
        P("chan"),
        P(("groups", "ctx"), "chan"),
    )
    out_specs = (
        P(("groups", "ctx"), "chan"),
        P(("groups", "ctx"), "chan"),
        P(("groups", "ctx"), "chan"),
        P(("groups", "ctx"), "chan"),
        P(("groups", "chan")),
    )
    return jax.shard_map(local, mesh=mesh, in_specs=in_specs, out_specs=out_specs, check_vma=False)
```

profile of v0, /device:TPU:0, one launch (start us, length us, event | category | flops | bytes accessed | tf_op | source)
XLA Modules:
  0.0 386.1 jit_solution(120343839279487304)
XLA Ops:
  7.2 4.2 %sine_negate_fusion.2 = (f32[513,512]{1,0:T(8,128)S(1)}, f32[513,512]{1,0:T(8,128)S(1)}) fusion(), kind=kLoop, calls=%fused_computation.105 | loop fusion | flops 3939840 | bytes 2101248 | tf_op jit(solution)/shard_map/neg | solution.py:18
  11.4 2.9 convolution_bitcast_fusion.3
  14.4 0.6 all-gather.9.cloned.1.call-start
  14.9 4.2 %fusion.71 = (f32[513,512]{1,0:T(8,128)S(1)}, f32[513,512]{1,0:T(8,128)S(1)}) fusion(s32[512]{0:T(512)S(1)} %iota_add_fusion), kind=kLoop, calls=%fused_computation.112 | loop fusion | flops 3939840 | bytes 2103296 | tf_op jit(solution)/shard_map/cos | solution.py:18
  19.1 2.8 fusion.32
  22.0 1.4 reduce-scatter.2.cloned.1.call-start
  23.5 8.4 %sine_negate_fusion = (f32[513,1024]{1,0:T(8,128)S(1)}, f32[513,1024]{1,0:T(8,128)S(1)}) fusion(), kind=kLoop, calls=%fused_computation.54 | loop fusion | flops 7879680 | bytes 4202496 | tf_op jit(solution)/shard_map/neg | solution.py:18
  31.8 10.6 %sine_multiply_fusion = (f32[1024,513]{1,0:T(8,128)S(1)}, f32[1024,513]{1,0:T(8,128)S(1)}) fusion(f32[513]{0:T(1024)S(1)} %fusion.73, f32[513]{0:T(1024)S(1)} %select_multiply_fusion), kind=kLoop, calls=%fused_computation.38 | loop fusion | flops 8404992 | bytes 4206600 | tf_op jit(solution)/shard_map/mul | solution.py:28
  42.4 2.5 pad_maximum_fusion.1
  44.9 2.9 pad_maximum_fusion
  47.9 50.6 %all-gather.7.cloned.1.call-done = f32[4,1026,256]{2,1,0:T(8,128)} async-done(((f32[1,1026,256]{2,1,0:T(8,128)}), f32[4,1026,256]{2,1,0:T(8,128)}) %all-gather.7.cloned.1.call-update) | async-done | bytes 4202512 | tf_op jit(solution)/shard_map/all_gather | solution.py:94
  98.5 81.4 %all-gather.9.cloned.1.call-done = f32[4,1026,256]{2,1,0:T(8,128)} async-done(((f32[1,1026,256]{2,1,0:T(8,128)}), f32[4,1026,256]{2,1,0:T(8,128)}) %all-gather.9.cloned.1.call-update) | async-done | bytes 4202512 | tf_op jit(solution)/shard_map/all_gather | solution.py:95
  179.9 2.3 broadcast_in_dim.27.clone
  182.2 121.5 %while.21 = (s32[]{:T(128)}, f32[1026,256]{1,0:T(8,128)}, f32[1026,256]{1,0:T(8,128)}, f32[4096,256]{1,0:T(8,128)}, s32[]{:T(128)}, /*index=5*/f32[4096,256]{1,0...) while((s32[]{:T(128)}, f32[1026,256]{1,0:T(8,128)}, ...), condition=%wide.region_1.2_spmd.clone, body=%wide.region_0.1_spmd.clone.sunk | while | flops 9687015424 | bytes 64113172 | solution.py:101
  182.6 5.7 %convolution_bitcast_fusion.6 = f32[1026,256]{1,0:T(8,128)S(1)} fusion(f32[1026,1024]{1,0:T(8,128)} %get-tuple-element.519, f32[4096,256]{1,0:T(8,128)} %get-tuple-element.518, s32[]{:T(128)S(6)} %select_n.167), kind=kOutput, calls=%fused_computation.1.clone.1 | convolution fusion | flops 3227516928 | bytes 6326276 | tf_op jit(solution)/shard_map/while/body/eval_jaxpr/dot_general | solution.py:9
  188.3 1.6 multiply_add_fusion.5
  189.9 5.7 %convolution_bitcast_fusion.7 = f32[1026,256]{1,0:T(8,128)S(1)} fusion(f32[1026,1024]{1,0:T(8,128)} %get-tuple-element.519, f32[4096,256]{1,0:T(8,128)} %get-tuple-element.518, s32[]{:T(128)S(6)} %select_n.168), kind=kOutput, calls=%fused_computation.clone.1 | convolution fusion | flops 3227516928 | bytes 6326276 | tf_op jit(solution)/shard_map/while/body/eval_jaxpr/dot_general | solution.py:9
  195.6 1.6 multiply_add_fusion.6
  197.5 0.6 maximum_add_fusion.3
  198.1 1.0 copy-done.3
  199.1 0.3 copy-done.6
  199.4 1.3 constant_dynamic-slice_fusion.2
  200.7 0.3 copy.19
  201.1 9.8 %fusion.98 = f32[1024,256]{0,1:T(8,128)S(1)} fusion(f32[1024,256]{0,1:T(8,128)S(1)} %copy.19, f32[1024,1026]{1,0:T(8,128)} %get-tuple-element.523, f32[513,256]{1,0:T(8,128)S(1)} %get-tuple-element.475, f32[513,256]{1,0:T(8,128)S(1)} %get-tuple-element.476), kind=kOutput, calls=%fused_computation.3.clone.1 | convolution fusion | flops 3228041728 | bytes 7350272 | tf_op jit(solution)/shard_map/while/body/eval_jaxpr/dot_general | solution.py:9
  211.3 1.1 constant_dynamic-update-slice_fusion.2
  212.3 0.5 copy-done.1
  212.9 5.7 %convolution_bitcast_fusion.6 = f32[1026,256]{1,0:T(8,128)S(1)} fusion(f32[1026,1024]{1,0:T(8,128)} %get-tuple-element.519, f32[4096,256]{1,0:T(8,128)} %get-tuple-element.518, s32[]{:T(128)S(6)} %select_n.167), kind=kOutput, calls=%fused_computation.1.clone.1 | convolution fusion | flops 3227516928 | bytes 6326276 | tf_op jit(solution)/shard_map/while/body/eval_jaxpr/dot_general | solution.py:9
  218.6 1.6 multiply_add_fusion.5
  220.2 5.7 %convolution_bitcast_fusion.7 = f32[1026,256]{1,0:T(8,128)S(1)} fusion(f32[1026,1024]{1,0:T(8,128)} %get-tuple-element.519, f32[4096,256]{1,0:T(8,128)} %get-tuple-element.518, s32[]{:T(128)S(6)} %select_n.168), kind=kOutput, calls=%fused_computation.clone.1 | convolution fusion | flops 3227516928 | bytes 6326276 | tf_op jit(solution)/shard_map/while/body/eval_jaxpr/dot_general | solution.py:9
  225.9 1.6 multiply_add_fusion.6
  227.7 0.6 maximum_add_fusion.3
  228.4 1.0 copy-done.3
  229.4 0.3 copy-done.6
  229.7 1.3 constant_dynamic-slice_fusion.2
  231.3 9.8 %fusion.98 = f32[1024,256]{0,1:T(8,128)S(1)} fusion(f32[1024,256]{0,1:T(8,128)S(1)} %copy.19, f32[1024,1026]{1,0:T(8,128)} %get-tuple-element.523, f32[513,256]{1,0:T(8,128)S(1)} %get-tuple-element.475, f32[513,256]{1,0:T(8,128)S(1)} %get-tuple-element.476), kind=kOutput, calls=%fused_computation.3.clone.1 | convolution fusion | flops 3228041728 | bytes 7350272 | tf_op jit(solution)/shard_map/while/body/eval_jaxpr/dot_general | solution.py:9
  241.5 1.1 constant_dynamic-update-slice_fusion.2
  242.6 0.5 copy-done.1
  243.1 5.7 %convolution_bitcast_fusion.6 = f32[1026,256]{1,0:T(8,128)S(1)} fusion(f32[1026,1024]{1,0:T(8,128)} %get-tuple-element.519, f32[4096,256]{1,0:T(8,128)} %get-tuple-element.518, s32[]{:T(128)S(6)} %select_n.167), kind=kOutput, calls=%fused_computation.1.clone.1 | convolution fusion | flops 3227516928 | bytes 6326276 | tf_op jit(solution)/shard_map/while/body/eval_jaxpr/dot_general | solution.py:9
  248.8 1.6 multiply_add_fusion.5
  250.4 5.7 %convolution_bitcast_fusion.7 = f32[1026,256]{1,0:T(8,128)S(1)} fusion(f32[1026,1024]{1,0:T(8,128)} %get-tuple-element.519, f32[4096,256]{1,0:T(8,128)} %get-tuple-element.518, s32[]{:T(128)S(6)} %select_n.168), kind=kOutput, calls=%fused_computation.clone.1 | convolution fusion | flops 3227516928 | bytes 6326276 | tf_op jit(solution)/shard_map/while/body/eval_jaxpr/dot_general | solution.py:9
  256.1 1.6 multiply_add_fusion.6
  258.0 0.6 maximum_add_fusion.3
  258.6 1.0 copy-done.3
  259.6 0.3 copy-done.6
  260.0 1.3 constant_dynamic-slice_fusion.2
  261.6 9.8 %fusion.98 = f32[1024,256]{0,1:T(8,128)S(1)} fusion(f32[1024,256]{0,1:T(8,128)S(1)} %copy.19, f32[1024,1026]{1,0:T(8,128)} %get-tuple-element.523, f32[513,256]{1,0:T(8,128)S(1)} %get-tuple-element.475, f32[513,256]{1,0:T(8,128)S(1)} %get-tuple-element.476), kind=kOutput, calls=%fused_computation.3.clone.1 | convolution fusion | flops 3228041728 | bytes 7350272 | tf_op jit(solution)/shard_map/while/body/eval_jaxpr/dot_general | solution.py:9
  271.8 1.0 constant_dynamic-update-slice_fusion.2
  272.8 0.6 copy-done.1
  273.4 5.7 %convolution_bitcast_fusion.6 = f32[1026,256]{1,0:T(8,128)S(1)} fusion(f32[1026,1024]{1,0:T(8,128)} %get-tuple-element.519, f32[4096,256]{1,0:T(8,128)} %get-tuple-element.518, s32[]{:T(128)S(6)} %select_n.167), kind=kOutput, calls=%fused_computation.1.clone.1 | convolution fusion | flops 3227516928 | bytes 6326276 | tf_op jit(solution)/shard_map/while/body/eval_jaxpr/dot_general | solution.py:9
  279.1 1.6 multiply_add_fusion.5
  280.7 5.7 %convolution_bitcast_fusion.7 = f32[1026,256]{1,0:T(8,128)S(1)} fusion(f32[1026,1024]{1,0:T(8,128)} %get-tuple-element.519, f32[4096,256]{1,0:T(8,128)} %get-tuple-element.518, s32[]{:T(128)S(6)} %select_n.168), kind=kOutput, calls=%fused_computation.clone.1 | convolution fusion | flops 3227516928 | bytes 6326276 | tf_op jit(solution)/shard_map/while/body/eval_jaxpr/dot_general | solution.py:9
  286.4 1.6 multiply_add_fusion.6
  288.3 0.6 maximum_add_fusion.3
  288.9 1.0 copy-done.3
  289.9 0.3 copy-done.6
  290.2 1.3 constant_dynamic-slice_fusion.2
  291.9 9.8 %fusion.98 = f32[1024,256]{0,1:T(8,128)S(1)} fusion(f32[1024,256]{0,1:T(8,128)S(1)} %copy.19, f32[1024,1026]{1,0:T(8,128)} %get-tuple-element.523, f32[513,256]{1,0:T(8,128)S(1)} %get-tuple-element.475, f32[513,256]{1,0:T(8,128)S(1)} %get-tuple-element.476), kind=kOutput, calls=%fused_computation.3.clone.1 | convolution fusion | flops 3228041728 | bytes 7350272 | tf_op jit(solution)/shard_map/while/body/eval_jaxpr/dot_general | solution.py:9
  302.0 1.1 constant_dynamic-update-slice_fusion.2
  303.1 0.5 copy-done.1
  303.7 11.6 %sine_multiply_fusion.1 = (f32[512,513]{1,0:T(8,128)S(1)}, f32[512,513]{1,0:T(8,128)S(1)}, f32[512,513]{1,0:T(8,128)}, f32[512,513]{1,0:T(8,128)S(1)}) fusion(f32[513]{0:T(1024)S(1)} %fusion.73, s32[512]{0:T(512)S(1)} %iota_add_fusion, f32[513]{0:T(1024)S(1)} %select_multiply_fusion), kind=kLoop, calls=%fused_computation.83 | loop fusion | flops 8404992 | bytes 4208648 | tf_op jit(solution)/shard_map/mul | solution.py:28
  315.3 3.4 multiply_reduce_fusion
  318.7 9.7 %psum.7 = f32[256]{0:T(256)} all-reduce(f32[256]{0:T(256)S(1)} %get-tuple-element.376), channel_id=1, replica_groups=mesh['groups'=2,'ctx'=4,'chan'=4] {'ctx'}, use_global_device_ids=true, to_apply=%region_4.5 | all-reduce | flops 256 | bytes 2048 | tf_op jit(solution)/shard_map/psum | solution.py:109
  328.4 4.6 %fusion.54 = f32[512,256]{1,0:T(8,128)} fusion(f32[512,256]{1,0:T(8,128)S(1)} %copy-done.9, f32[1026,256]{1,0:T(8,128)S(1)} %copy-done.7, f32[512,513]{1,0:T(8,128)S(1)} %get-tuple-element.382, f32[512,513]{1,0:T(8,128)} %get-tuple-element.390, f32[256]{0:T(256)S(1)} %copy-done.16, f32[512,256]{1,0:T(8,128)S(1)} %copy-done.11, f32[512,256]{1,0:T(8,128)} %param.10), kind=kOutput, calls=%fused_computation.95 | convolution fusion | flops 1614808064 | bytes 5250048 | tf_op jit(solution)/shard_map/dot_general | solution.py:9
  333.1 46.3 %reduce-scatter.2.cloned.1.call-done = f32[1024,256]{1,0:T(8,128)} async-done(((f32[4096,256]{1,0:T(8,128)}), f32[1024,256]{1,0:T(8,128)}) %reduce-scatter.2.cloned.1.call-update) | async-done | bytes 1048592 | tf_op jit(solution)/shard_map/reduce_scatter | solution.py:103
  (68 shorter events, 3.5 us)
Async XLA Ops:
  7.2 4.3 %copy-start.10 = (f32[512,256]{1,0:T(8,128)S(1)}, f32[512,256]{1,0:T(8,128)}, u32[]{:S(2)}) copy-start(f32[512,256]{1,0:T(8,128)} %param.9) | copy-start | bytes 1572868
  7.2 4.3 %copy-start.12 = (f32[512,256]{1,0:T(8,128)S(1)}, f32[512,256]{1,0:T(8,128)}, u32[]{:S(2)}) copy-start(f32[512,256]{1,0:T(8,128)} %param.10) | copy-start | bytes 1572868
  7.2 91.3 %all-gather.7.cloned.1.call-start = ((), (), s32[]{:S(2)}) async-start(), calls=%async_computation.2 | async-start | bytes 5283840 | tf_op jit(solution)/shard_map/all_gather | solution.py:94
  14.3 4.8 %copy-start.8 = (f32[512,256]{1,0:T(8,128)S(1)}, f32[512,256]{1,0:T(8,128)}, u32[]{:S(2)}) copy-start(f32[512,256]{1,0:T(8,128)} %param.13) | copy-start | bytes 1572868
  14.3 4.8 %copy-start.14 = (f32[512,256]{1,0:T(8,128)S(1)}, f32[512,256]{1,0:T(8,128)}, u32[]{:S(2)}) copy-start(f32[512,256]{1,0:T(8,128)} %param.8) | copy-start | bytes 1572868
  14.4 165.6 %all-gather.9.cloned.1.call-start = ((), (), s32[]{:S(2)}) async-start(), calls=%async_computation.3 | async-start | bytes 5283840 | tf_op jit(solution)/shard_map/all_gather | solution.py:95
  22.0 357.4 %reduce-scatter.2.cloned.1.call-start = ((), (), s32[]{:S(2)}) async-start(), calls=%async_computation.1 | async-start | bytes 5242880 | tf_op jit(solution)/shard_map/reduce_scatter | solution.py:103
  47.9 134.3 %copy-start = (f32[1026,256]{1,0:T(8,128)S(1)}, f32[1026,256]{1,0:T(8,128)}, u32[]{:S(2)}) copy-start(f32[1026,256]{1,0:T(8,128)} %fusion.32) | copy-start | bytes 3151876
  195.6 1.6 copy-start.2
  195.6 1.9 copy-start.5
  198.1 1.0 copy-start.3
  198.1 1.3 copy-start.6
  211.3 1.6 copy-start.1
  225.9 1.6 copy-start.2
  225.9 1.9 copy-start.5
  228.4 1.0 copy-start.3
  228.4 1.3 copy-start.6
  241.5 1.6 copy-start.1
  256.1 1.6 copy-start.2
  256.1 1.9 copy-start.5
  258.6 1.0 copy-start.3
  258.6 1.3 copy-start.6
  271.8 1.6 copy-start.1
  286.4 1.6 copy-start.2
  286.4 1.9 copy-start.5
  288.9 1.0 copy-start.3
  288.9 1.3 copy-start.6
  302.0 1.6 copy-start.1
  303.7 11.6 %copy-start.4 = (f32[1026,256]{1,0:T(8,128)S(1)}, f32[1026,256]{1,0:T(8,128)}, u32[]{:S(2)}) copy-start(f32[1026,256]{1,0:T(8,128)} %get-tuple-element.538) | copy-start | bytes 3151876
  303.7 11.6 %copy-start.9 = (f32[512,256]{1,0:T(8,128)S(1)}, f32[512,256]{1,0:T(8,128)}, u32[]{:S(2)}) copy-start(f32[512,256]{1,0:T(8,128)} %param.13) | copy-start | bytes 1572868
  303.7 11.6 %copy-start.11 = (f32[512,256]{1,0:T(8,128)S(1)}, f32[512,256]{1,0:T(8,128)}, u32[]{:S(2)}) copy-start(f32[512,256]{1,0:T(8,128)} %param.9) | copy-start | bytes 1572868
  303.7 11.6 %copy-start.13 = (f32[512,256]{1,0:T(8,128)S(1)}, f32[512,256]{1,0:T(8,128)}, u32[]{:S(2)}) copy-start(f32[512,256]{1,0:T(8,128)} %param.10) | copy-start | bytes 1572868
  303.7 11.6 %copy-start.15 = (f32[512,256]{1,0:T(8,128)S(1)}, f32[512,256]{1,0:T(8,128)}, u32[]{:S(2)}) copy-start(f32[512,256]{1,0:T(8,128)} %param.8) | copy-start | bytes 1572868
  303.7 11.6 %copy-start.16 = (f32[256]{0:T(256)S(1)}, f32[256]{0:T(256)}, u32[]{:S(2)}) copy-start(f32[256]{0:T(256)} %param.12) | copy-start | bytes 3076
  315.3 13.1 %copy-start.7 = (f32[1026,256]{1,0:T(8,128)S(1)}, f32[1026,256]{1,0:T(8,128)}, u32[]{:S(2)}) copy-start(f32[1026,256]{1,0:T(8,128)} %get-tuple-element.537) | copy-start | bytes 3151876
Sparse Core Ops, SparseCore 0:
  14.4 83.9 all-gather.6
  100.0 79.8 all-gather.8
  303.8 75.5 reduce-scatter.1
where the time goes:
time: 392 us; the launch traced here: 386 us
  waiting for transfers between devices  178 us (45%)
  matrix products  98.5 us (25%)
  other arithmetic  59.7 us (15%)
  local copies, waits for them, and re-layouts  22.8 us (6%)
  between operations  14.1 us (4%)
  blocking collectives  9.73 us (2%)
    dot_general x16, matrix products, matmul(): jnp.dot(left, right, preferred_element_type=jnp.float32, precision=lax.Pr...  98.5 us
    all_gather x1, waiting for transfers between devices, local(): lax.all_gather(own_grad_spec[None], 'ctx', axis=0, tiled=True)  81.4 us
    all_gather x1, waiting for transfers between devices, local(): lax.all_gather(own_gated_spec[None], 'ctx', axis=0, tiled=True)  50.6 us
    reduce_scatter x1, waiting for transfers between devices, local(): lax.psum_scatter(partial_value, 'ctx', scatter_dimension=0, tiled=True)  46.3 us
    mul x2, other arithmetic, inverse_table(): -weights * jnp.sin(angles)  22.1 us
    add x8, other arithmetic, conj_times(): real_a * real_b + imag_a * imag_b  12.8 us
    neg x2, other arithmetic, forward_table(): return jnp.concatenate([jnp.cos(angles), -jnp.sin(angles)], axis=0)  12.5 us
    psum x1, blocking collectives, local(): skip_grad = lax.psum(jnp.sum(mixed_grad * gated, axis=0), 'ctx')  9.73 us
  transfers between devices with their start and end apart: 3, of which 3 were waited for; matrix products, arithmetic and copies ran while one was open for 13% of the time, Pallas kernels for 0%

commit v1 on v0

--- a/solution.py
+++ b/solution.py
@@ -3,6 +3,29 @@
 import jax.numpy as jnp
 from jax import lax
 from jax.sharding import PartitionSpec as P
+
+
+def _enter_tokens(q_in):
+    field_out = jax.lax.axis_size("ctx")
+    everything = jax.lax.axis_index("ctx")
+    t1, placed, formed = (field_out, everything, q_in.shape[0])
+    pages = [(jj, (jj + 1) % t1) for jj in range(t1)]
+    in_order = [(jj, (jj - 1) % t1) for jj in range(t1)]
+    frame_out = jnp.zeros((*q_in.shape[:0], t1 * formed, *q_in.shape[1:]), q_in.dtype)
+    frame_out = lax.dynamic_update_slice_in_dim(frame_out, q_in, placed * formed, axis=0)
+    after = piece_out = q_in
+    long_array = t1 // 2
+    for rr in range(1, long_array + 1):
+        after = jax.lax.ppermute(after, "ctx", pages)
+        frame_out = lax.dynamic_update_slice_in_dim(
+            frame_out, after, (placed - rr) % t1 * formed, axis=0
+        )
+        if rr < t1 - long_array:
+            piece_out = jax.lax.ppermute(piece_out, "ctx", in_order)
+            frame_out = lax.dynamic_update_slice_in_dim(
+                frame_out, piece_out, (placed + rr) % t1 * formed, axis=0
+            )
+    return frame_out
 
 
 def matmul(left, right):
@@ -91,7 +114,7 @@
     )
     own_gated_spec = matmul(table_low, gated)
     pieces = (
-        lax.all_gather(own_gated_spec[None], "ctx", axis=0, tiled=True),
+        _enter_tokens(own_gated_spec[None]),
         lax.all_gather(own_grad_spec[None], "ctx", axis=0, tiled=True),
     )
 

time: 392 us -> 378 us (0.964)
  waiting for transfers between devices: 178 us -> 105 us
  starting transfers between devices: 2.02 us -> 48.5 us
  local copies, waits for them, and re-layouts: 22.8 us -> 33.1 us
    all_gather x1, waiting for transfers between devices: 81.4 us -> 0.01 us  [local(): lax.all_gather(own_grad_spec[None], 'ctx', axis=0, tiled=True)]
    ppermute x0 -> x3, waiting for transfers between devices: none -> 58.7 us  [the longest x2 57.4 us: _enter_tokens(): after = jax.lax.ppermute(after, 'ctx', pages)]
    all_gather x1 -> x0, waiting for transfers between devices: 50.6 us -> none  [local(): lax.all_gather(own_gated_spec[None], 'ctx', axis=0, tiled=True)]
    ppermute x0 -> x3, starting transfers between devices: none -> 47.9 us  [the longest x2 45.6 us: _enter_tokens(): after = jax.lax.ppermute(after, 'ctx', pages)]
    broadcast_in_dim x0 -> x2, local copies, waits for them, and re-layouts: none -> 6.89 us  [the longest x1 4.58 us: local(): own_gated_spec[None]]
  transfers between devices with their start and end apart: 3 -> 5, of which waited for: 3 -> 4; matrix products, arithmetic and copies ran while one was open for 13% -> 17% of each run, Pallas kernels for 0% -> 0%
where the time goes in v1:
time: 378 us; the launch traced here: 372 us
  waiting for transfers between devices  105 us (28%)
  matrix products  98.6 us (26%)
  other arithmetic  63 us (17%)
  starting transfers between devices  48.5 us (13%)
  local copies, waits for them, and re-layouts  33.1 us (9%)
  between operations  14.5 us (4%)
  blocking collectives  9.58 us (3%)
    dot_general x16, matrix products, matmul(): jnp.dot(left, right, preferred_element_type=jnp.float32, precision=lax.Pr...  98.6 us
    ppermute x2, waiting for transfers between devices, _enter_tokens(): after = jax.lax.ppermute(after, 'ctx', pages)  57.4 us
    reduce_scatter x1, waiting for transfers between devices, local(): lax.psum_scatter(partial_value, 'ctx', scatter_dimension=0, tiled=True)  45.8 us
    ppermute x2, starting transfers between devices, _enter_tokens(): after = jax.lax.ppermute(after, 'ctx', pages)  45.6 us
    mul x2, other arithmetic, inverse_table(): -weights * jnp.sin(angles)  23.2 us
    neg x2, other arithmetic, forward_table(): return jnp.concatenate([jnp.cos(angles), -jnp.sin(angles)], axis=0)  12.5 us
    add x8, other arithmetic, conj_times(): real_a * real_b + imag_a * imag_b  12.3 us
    psum x1, blocking collectives, local(): skip_grad = lax.psum(jnp.sum(mixed_grad * gated, axis=0), 'ctx')  9.58 us
  transfers between devices with their start and end apart: 5, of which 4 were waited for; matrix products, arithmetic and copies ran while one was open for 17% of the time, Pallas kernels for 0%

profile of v1, /device:TPU:0, one launch (start us, length us, event | category | flops | bytes accessed | tf_op | source)
XLA Modules:
  0.0 372.2 jit_solution(119328479816475116)
XLA Ops:
  7.2 4.2 %fusion.71 = (f32[513,512]{1,0:T(8,128)S(1)}, f32[513,512]{1,0:T(8,128)S(1)}) fusion(s32[512]{0:T(512)S(1)} %iota_add_fusion), kind=kLoop, calls=%fused_computation.115 | loop fusion | flops 3939840 | bytes 2103296 | tf_op jit(solution)/shard_map/cos | solution.py:41
  11.5 2.8 fusion.32
  14.3 0.6 reduce-scatter.2.cloned.1.call-start
  14.9 4.2 %sine_negate_fusion.2 = (f32[513,512]{1,0:T(8,128)S(1)}, f32[513,512]{1,0:T(8,128)S(1)}) fusion(), kind=kLoop, calls=%fused_computation.105 | loop fusion | flops 3939840 | bytes 2101248 | tf_op jit(solution)/shard_map/neg | solution.py:41
  19.1 2.3 broadcast_in_dim.31
  21.4 2.8 constant_dynamic-update-slice_fusion.1
  24.2 4.6 %copy.12 = f32[1,1026,256]{2,0,1:T(1,128)S(1)} copy(f32[1,1026,256]{2,1,0:T(8,128)S(1)} %get-tuple-element.386) | data formatting | bytes 2101248 | tf_op jit(solution)/shard_map/broadcast_in_dim | solution.py:117
  28.8 3.1 collective-permute-start
  31.9 2.3 collective-permute-start.1
  34.2 8.4 %sine_negate_fusion = (f32[513,1024]{1,0:T(8,128)S(1)}, f32[513,1024]{1,0:T(8,128)S(1)}) fusion(), kind=kLoop, calls=%fused_computation.54 | loop fusion | flops 7879680 | bytes 4202496 | tf_op jit(solution)/shard_map/neg | solution.py:41
  42.5 2.7 pad_maximum_fusion.1
  45.2 11.6 %sine_multiply_fusion = (f32[1024,513]{1,0:T(8,128)}, f32[1024,513]{1,0:T(8,128)}) fusion(f32[513]{0:T(1024)S(1)} %fusion.73, f32[513]{0:T(1024)S(1)} %select_multiply_fusion), kind=kLoop, calls=%fused_computation.38 | loop fusion | flops 8404992 | bytes 4206600 | tf_op jit(solution)/shard_map/mul | solution.py:51
  56.8 5.5 %pad_maximum_fusion = f32[1024,1026]{1,0:T(8,128)} fusion(f32[1024,513]{1,0:T(8,128)} %get-tuple-element.394, f32[1024,513]{1,0:T(8,128)} %get-tuple-element.395), kind=kLoop, calls=%fused_computation.26 | loop fusion | flops 1050624 | bytes 8404992 | tf_op jit(solution)/shard_map/concatenate | solution.py:51
  62.3 18.2 %collective-permute-done = f32[1,1026,256]{2,0,1:T(1,128)S(1)} collective-permute-done((f32[1,1026,256]{2,0,1:T(1,128)S(1)}, f32[1,1026,256]{2,0,1:T(1,128)S(1)}, u32[]{:S(2)}, u32[]{:S(2)}) %collective-permute-start) | collective-permute-done | bytes 1050656 | tf_op jit(solution)/shard_map/ppermute | solution.py:19
  80.5 42.5 %collective-permute-start.2 = (f32[1,1026,256]{2,0,1:T(1,128)S(1)}, f32[1,1026,256]{2,0,1:T(1,128)S(1)}, u32[]{:S(2)}, u32[]{:S(2)}) collective-permute-start(f32[1,1026,256]{2,0,1:T(1,128)S(1)} %collective-permute-done), channel_id=1, source_target_pairs={{0,4},{4,8},{8,12},{12,0},{1,5},{5,9},{9,13},{13,1},{2,6},{6,10},{... | collective-permute-start | bytes 3151880 | tf_op jit(solution)/shard_map/ppermute | solution.py:19
  123.0 1.0 copy_dynamic-update-slice_fusion.2
  124.0 1.2 collective-permute-done.1
  125.3 1.1 copy_dynamic-update-slice_fusion.1
  126.3 39.2 %collective-permute-done.2 = f32[1,1026,256]{2,0,1:T(1,128)S(1)} collective-permute-done((f32[1,1026,256]{2,0,1:T(1,128)S(1)}, f32[1,1026,256]{2,0,1:T(1,128)S(1)}, u32[]{:S(2)}, u32[]{:S(2)}) %collective-permute-start.2) | collective-permute-done | bytes 1050656 | tf_op jit(solution)/shard_map/ppermute | solution.py:19
  165.6 1.1 copy_dynamic-update-slice_fusion
  166.6 2.3 broadcast_in_dim.30.clone
  168.9 120.8 %while.21 = (s32[]{:T(128)}, f32[1026,256]{1,0:T(8,128)}, f32[1026,256]{1,0:T(8,128)}, f32[4096,256]{1,0:T(8,128)}, s32[]{:T(128)}, /*index=5*/f32[4096,256]{1,0...) while((s32[]{:T(128)}, f32[1026,256]{1,0:T(8,128)}, ...), condition=%wide.region_1.2_spmd.clone, body=%wide.region_0.1_spmd.clone.sunk | while | flops 9687015424 | bytes 64113172 | solution.py:124
  168.9 5.7 %convolution_bitcast_fusion.6 = f32[1026,256]{1,0:T(8,128)S(1)} fusion(f32[1026,1024]{1,0:T(8,128)} %get-tuple-element.521, f32[4096,256]{1,0:T(8,128)} %get-tuple-element.520, s32[]{:T(128)S(6)} %select_n.200), kind=kOutput, calls=%fused_computation.1.clone.1 | convolution fusion | flops 3227516928 | bytes 6326276 | tf_op jit(solution)/shard_map/while/body/eval_jaxpr/dot_general | solution.py:32
  174.6 1.5 multiply_add_fusion.5
  176.1 5.7 %convolution_bitcast_fusion.7 = f32[1026,256]{1,0:T(8,128)S(1)} fusion(f32[1026,1024]{1,0:T(8,128)} %get-tuple-element.521, f32[4096,256]{1,0:T(8,128)} %get-tuple-element.520, s32[]{:T(128)S(6)} %select_n.201), kind=kOutput, calls=%fused_computation.clone.1 | convolution fusion | flops 3227516928 | bytes 6326276 | tf_op jit(solution)/shard_map/while/body/eval_jaxpr/dot_general | solution.py:32
  181.9 1.5 multiply_add_fusion.6
  183.7 0.6 maximum_add_fusion.3
  184.4 1.0 copy-done.3
  185.7 1.3 constant_dynamic-slice_fusion.2
  187.3 9.8 %fusion.98 = f32[1024,256]{0,1:T(8,128)S(1)} fusion(f32[1024,256]{0,1:T(8,128)S(1)} %copy.27, f32[1024,1026]{1,0:T(8,128)} %get-tuple-element.525, f32[513,256]{1,0:T(8,128)S(1)} %get-tuple-element.477, f32[513,256]{1,0:T(8,128)S(1)} %get-tuple-element.478), kind=kOutput, calls=%fused_computation.3.clone.1 | convolution fusion | flops 3228041728 | bytes 7350272 | tf_op jit(solution)/shard_map/while/body/eval_jaxpr/dot_general | solution.py:32
  197.5 1.1 constant_dynamic-update-slice_fusion.3
  199.1 5.7 %convolution_bitcast_fusion.6 = f32[1026,256]{1,0:T(8,128)S(1)} fusion(f32[1026,1024]{1,0:T(8,128)} %get-tuple-element.521, f32[4096,256]{1,0:T(8,128)} %get-tuple-element.520, s32[]{:T(128)S(6)} %select_n.200), kind=kOutput, calls=%fused_computation.1.clone.1 | convolution fusion | flops 3227516928 | bytes 6326276 | tf_op jit(solution)/shard_map/while/body/eval_jaxpr/dot_general | solution.py:32
  204.8 1.5 multiply_add_fusion.5
  206.3 5.7 %convolution_bitcast_fusion.7 = f32[1026,256]{1,0:T(8,128)S(1)} fusion(f32[1026,1024]{1,0:T(8,128)} %get-tuple-element.521, f32[4096,256]{1,0:T(8,128)} %get-tuple-element.520, s32[]{:T(128)S(6)} %select_n.201), kind=kOutput, calls=%fused_computation.clone.1 | convolution fusion | flops 3227516928 | bytes 6326276 | tf_op jit(solution)/shard_map/while/body/eval_jaxpr/dot_general | solution.py:32
  212.1 1.5 multiply_add_fusion.6
  213.9 0.6 maximum_add_fusion.3
  214.6 1.0 copy-done.3
  215.9 1.3 constant_dynamic-slice_fusion.2
  217.5 9.8 %fusion.98 = f32[1024,256]{0,1:T(8,128)S(1)} fusion(f32[1024,256]{0,1:T(8,128)S(1)} %copy.27, f32[1024,1026]{1,0:T(8,128)} %get-tuple-element.525, f32[513,256]{1,0:T(8,128)S(1)} %get-tuple-element.477, f32[513,256]{1,0:T(8,128)S(1)} %get-tuple-element.478), kind=kOutput, calls=%fused_computation.3.clone.1 | convolution fusion | flops 3228041728 | bytes 7350272 | tf_op jit(solution)/shard_map/while/body/eval_jaxpr/dot_general | solution.py:32
  227.7 1.1 constant_dynamic-update-slice_fusion.3
  229.3 5.7 %convolution_bitcast_fusion.6 = f32[1026,256]{1,0:T(8,128)S(1)} fusion(f32[1026,1024]{1,0:T(8,128)} %get-tuple-element.521, f32[4096,256]{1,0:T(8,128)} %get-tuple-element.520, s32[]{:T(128)S(6)} %select_n.200), kind=kOutput, calls=%fused_computation.1.clone.1 | convolution fusion | flops 3227516928 | bytes 6326276 | tf_op jit(solution)/shard_map/while/body/eval_jaxpr/dot_general | solution.py:32
  235.0 1.5 multiply_add_fusion.5
  236.5 5.7 %convolution_bitcast_fusion.7 = f32[1026,256]{1,0:T(8,128)S(1)} fusion(f32[1026,1024]{1,0:T(8,128)} %get-tuple-element.521, f32[4096,256]{1,0:T(8,128)} %get-tuple-element.520, s32[]{:T(128)S(6)} %select_n.201), kind=kOutput, calls=%fused_computation.clone.1 | convolution fusion | flops 3227516928 | bytes 6326276 | tf_op jit(solution)/shard_map/while/body/eval_jaxpr/dot_general | solution.py:32
  242.3 1.5 multiply_add_fusion.6
  244.1 0.6 maximum_add_fusion.3
  244.8 1.0 copy-done.3
  246.1 1.3 constant_dynamic-slice_fusion.2
  247.7 9.8 %fusion.98 = f32[1024,256]{0,1:T(8,128)S(1)} fusion(f32[1024,256]{0,1:T(8,128)S(1)} %copy.27, f32[1024,1026]{1,0:T(8,128)} %get-tuple-element.525, f32[513,256]{1,0:T(8,128)S(1)} %get-tuple-element.477, f32[513,256]{1,0:T(8,128)S(1)} %get-tuple-element.478), kind=kOutput, calls=%fused_computation.3.clone.1 | convolution fusion | flops 3228041728 | bytes 7350272 | tf_op jit(solution)/shard_map/while/body/eval_jaxpr/dot_general | solution.py:32
  257.9 1.0 constant_dynamic-update-slice_fusion.3
  258.9 0.6 copy-done.1
  259.5 5.7 %convolution_bitcast_fusion.6 = f32[1026,256]{1,0:T(8,128)S(1)} fusion(f32[1026,1024]{1,0:T(8,128)} %get-tuple-element.521, f32[4096,256]{1,0:T(8,128)} %get-tuple-element.520, s32[]{:T(128)S(6)} %select_n.200), kind=kOutput, calls=%fused_computation.1.clone.1 | convolution fusion | flops 3227516928 | bytes 6326276 | tf_op jit(solution)/shard_map/while/body/eval_jaxpr/dot_general | solution.py:32
  265.2 1.5 multiply_add_fusion.5
  266.7 5.7 %convolution_bitcast_fusion.7 = f32[1026,256]{1,0:T(8,128)S(1)} fusion(f32[1026,1024]{1,0:T(8,128)} %get-tuple-element.521, f32[4096,256]{1,0:T(8,128)} %get-tuple-element.520, s32[]{:T(128)S(6)} %select_n.201), kind=kOutput, calls=%fused_computation.clone.1 | convolution fusion | flops 3227516928 | bytes 6326276 | tf_op jit(solution)/shard_map/while/body/eval_jaxpr/dot_general | solution.py:32
  272.5 1.5 multiply_add_fusion.6
  274.3 0.6 maximum_add_fusion.3
  275.0 1.0 copy-done.3
  276.3 1.3 constant_dynamic-slice_fusion.2
  277.9 9.8 %fusion.98 = f32[1024,256]{0,1:T(8,128)S(1)} fusion(f32[1024,256]{0,1:T(8,128)S(1)} %copy.27, f32[1024,1026]{1,0:T(8,128)} %get-tuple-element.525, f32[513,256]{1,0:T(8,128)S(1)} %get-tuple-element.477, f32[513,256]{1,0:T(8,128)S(1)} %get-tuple-element.478), kind=kOutput, calls=%fused_computation.3.clone.1 | convolution fusion | flops 3228041728 | bytes 7350272 | tf_op jit(solution)/shard_map/while/body/eval_jaxpr/dot_general | solution.py:32
  288.1 1.1 constant_dynamic-update-slice_fusion.3
  289.8 11.6 %sine_multiply_fusion.1 = (f32[512,513]{1,0:T(8,128)S(1)}, f32[512,513]{1,0:T(8,128)S(1)}, f32[512,513]{1,0:T(8,128)}, f32[512,513]{1,0:T(8,128)S(1)}) fusion(f32[513]{0:T(1024)S(1)} %fusion.73, s32[512]{0:T(512)S(1)} %iota_add_fusion, f32[513]{0:T(1024)S(1)} %select_multiply_fusion), kind=kLoop, calls=%fused_computation.83 | loop fusion | flops 8404992 | bytes 4208648 | tf_op jit(solution)/shard_map/mul | solution.py:51
  301.5 3.3 multiply_reduce_fusion
  304.8 9.6 %psum.7 = f32[256]{0:T(256)} all-reduce(f32[256]{0:T(256)S(1)} %get-tuple-element.376), channel_id=1, replica_groups=mesh['groups'=2,'ctx'=4,'chan'=4] {'ctx'}, use_global_device_ids=true, to_apply=%region_4.5 | all-reduce | flops 256 | bytes 2048 | tf_op jit(solution)/shard_map/psum | solution.py:132
  314.4 4.9 %fusion.54 = f32[512,256]{1,0:T(8,128)} fusion(f32[512,256]{1,0:T(8,128)} %param.13, f32[1026,256]{1,0:T(8,128)S(1)} %copy-done.7, f32[512,513]{1,0:T(8,128)S(1)} %get-tuple-element.382, f32[512,513]{1,0:T(8,128)} %get-tuple-element.392, f32[256]{0:T(256)S(1)} %copy-done.16, f32[512,256]{1,0:T(8,128)} %param.9, f32[512,256]{1,0:T(8,128)} %param.10), kind=kOutput, calls=%fused_computation.95 | convolution fusion | flops 1614808064 | bytes 5250048 | tf_op jit(solution)/shard_map/dot_general | solution.py:32
  319.2 45.8 %reduce-scatter.2.cloned.1.call-done = f32[1024,256]{1,0:T(8,128)} async-done(((f32[4096,256]{1,0:T(8,128)}), f32[1024,256]{1,0:T(8,128)}) %reduce-scatter.2.cloned.1.call-update) | async-done | bytes 1048592 | tf_op jit(solution)/shard_map/reduce_scatter | solution.py:126
  (76 shorter events, 6.7 us)
Async XLA Ops:
  7.2 4.3 %copy-start.8 = (f32[512,256]{1,0:T(8,128)S(1)}, f32[512,256]{1,0:T(8,128)}, u32[]{:S(2)}) copy-start(f32[512,256]{1,0:T(8,128)} %param.13) | copy-start | bytes 1572868
  7.2 4.3 %copy-start.14 = (f32[512,256]{1,0:T(8,128)S(1)}, f32[512,256]{1,0:T(8,128)}, u32[]{:S(2)}) copy-start(f32[512,256]{1,0:T(8,128)} %param.8) | copy-start | bytes 1572868
  7.2 159.5 %all-gather.4.cloned.1.call-start = ((), (), s32[]{:S(2)}) async-start(), calls=%async_computation.2 | async-start | bytes 5283840 | tf_op jit(solution)/shard_map/all_gather | solution.py:118
  14.3 350.7 %reduce-scatter.2.cloned.1.call-start = ((), (), s32[]{:S(2)}) async-start(), calls=%async_computation.1 | async-start | bytes 5242880 | tf_op jit(solution)/shard_map/reduce_scatter | solution.py:126
  19.1 2.3 copy-start.10
  19.1 2.3 copy-start.12
  28.8 51.6 %collective-permute-start = (f32[1,1026,256]{2,0,1:T(1,128)S(1)}, f32[1,1026,256]{2,0,1:T(1,128)S(1)}, u32[]{:S(2)}, u32[]{:S(2)}) collective-permute-start(f32[1,1026,256]{2,0,1:T(1,128)S(1)} %copy.12), channel_id=1, source_target_pairs={{0,4},{4,8},{8,12},{12,0},{1,5},{5,9},{9,13},{13,1},{2,6},{6,10},{... | collective-permute-start | bytes 3151880 | tf_op jit(solution)/shard_map/ppermute | solution.py:19
  31.9 93.4 %collective-permute-start.1 = (f32[1,1026,256]{2,0,1:T(1,128)S(1)}, f32[1,1026,256]{2,0,1:T(1,128)S(1)}, u32[]{:S(2)}, u32[]{:S(2)}) collective-permute-start(f32[1,1026,256]{2,0,1:T(1,128)S(1)} %copy.12), channel_id=1, source_target_pairs={{0,12},{4,0},{8,4},{12,8},{1,13},{5,1},{9,5},{13,9},{2,14},{6,2},{... | collective-permute-start | bytes 3151880 | tf_op jit(solution)/shard_map/ppermute | solution.py:24
  80.5 85.1 %collective-permute-start.2 = (f32[1,1026,256]{2,0,1:T(1,128)S(1)}, f32[1,1026,256]{2,0,1:T(1,128)S(1)}, u32[]{:S(2)}, u32[]{:S(2)}) collective-permute-start(f32[1,1026,256]{2,0,1:T(1,128)S(1)} %collective-permute-done), channel_id=1, source_target_pairs={{0,4},{4,8},{8,12},{12,0},{1,5},{5,9},{9,13},{13,1},{2,6},{6,10},{... | collective-permute-start | bytes 3151880 | tf_op jit(solution)/shard_map/ppermute | solution.py:19
  166.6 2.3 copy-start
  181.8 1.6 copy-start.2
  181.9 1.9 copy-start.5
  184.3 1.0 copy-start.3
  184.4 1.3 copy-start.6
  197.5 1.6 copy-start.1
  212.0 1.6 copy-start.2
  212.0 1.9 copy-start.5
  214.5 1.0 copy-start.3
  214.6 1.3 copy-start.6
  227.7 1.6 copy-start.1
  242.2 1.6 copy-start.2
  242.2 1.9 copy-start.5
  244.7 1.0 copy-start.3
  244.7 1.3 copy-start.6
  257.9 1.6 copy-start.1
  272.4 1.6 copy-start.2
  272.4 1.9 copy-start.5
  274.9 1.0 copy-start.3
  274.9 1.3 copy-start.6
  288.1 1.6 copy-start.1
  289.7 11.7 %copy-start.4 = (f32[1026,256]{1,0:T(8,128)S(1)}, f32[1026,256]{1,0:T(8,128)}, u32[]{:S(2)}) copy-start(f32[1026,256]{1,0:T(8,128)} %get-tuple-element.539) | copy-start | bytes 3151876
  289.7 11.7 %copy-start.9 = (f32[512,256]{1,0:T(8,128)S(1)}, f32[512,256]{1,0:T(8,128)}, u32[]{:S(2)}) copy-start(f32[512,256]{1,0:T(8,128)} %param.13) | copy-start | bytes 1572868
  289.7 11.7 %copy-start.11 = (f32[512,256]{1,0:T(8,128)S(1)}, f32[512,256]{1,0:T(8,128)}, u32[]{:S(2)}) copy-start(f32[512,256]{1,0:T(8,128)} %param.9) | copy-start | bytes 1572868
  289.8 11.7 %copy-start.13 = (f32[512,256]{1,0:T(8,128)S(1)}, f32[512,256]{1,0:T(8,128)}, u32[]{:S(2)}) copy-start(f32[512,256]{1,0:T(8,128)} %param.10) | copy-start | bytes 1572868
  289.8 11.7 %copy-start.15 = (f32[512,256]{1,0:T(8,128)S(1)}, f32[512,256]{1,0:T(8,128)}, u32[]{:S(2)}) copy-start(f32[512,256]{1,0:T(8,128)} %param.8) | copy-start | bytes 1572868
  289.8 11.7 %copy-start.16 = (f32[256]{0:T(256)S(1)}, f32[256]{0:T(256)}, u32[]{:S(2)}) copy-start(f32[256]{0:T(256)} %param.12) | copy-start | bytes 3076
  301.5 12.9 %copy-start.7 = (f32[1026,256]{1,0:T(8,128)S(1)}, f32[1026,256]{1,0:T(8,128)}, u32[]{:S(2)}) copy-start(f32[1026,256]{1,0:T(8,128)} %get-tuple-element.538) | copy-start | bytes 3151876
Sparse Core Ops, SparseCore 0:
  14.4 143.8 all-gather.3
  289.8 75.1 reduce-scatter.1
